TPU v7x, 256 devices: a whole 4x4x8 slice. The times are simulated.
256 devices in a mesh: row: 8 (over z), col: 32 (over y, x, core).
Axes of the slice: x: 4, y: 4, z: 8, core: 2. Of those that a mesh axis runs over, the one named last changes fastest.
Arguments:
- blocks: bfloat16 [8, 32, 256, 128, 128], P('row', 'col'), may hold values from 0 to 0.0625
- slot_rows: int32 [8, 32, 256], P('row', 'col'), may hold values from 0 to 255, as said below
- slot_cols: int32 [8, 32, 256], P('row', 'col'), may hold values from 0 to 63, as said below
- counts: int32 [8, 32], P('row', 'col'), may hold values from 0 to 256, as said below
- reward_table: bfloat16 [32, 262144], P('row', 'col'), may hold values from -6 to 6
- reward_cols: int32 [16], replicated, may hold values from 0 to 31, as said below
- cotangent: bfloat16 [16, 262144], P(None, ('row', 'col')), may hold values from -6 to 6
Outputs:
- value: float32 [16, 262144], P(None, ('row', 'col'))
- grad: float32 [16, 262144], P('row', 'col')
Inputs may be any that keep to these rules, and one draw needn't show every extreme that they name: `counts`: stored blocks of each grid cell; along every grid row the cells of even index hold 2048 of them, and so do the cells of odd index, and some cell of every grid row holds exactly 256. Only the first counts[a, b] slots of a grid cell hold stored blocks; every block row has exactly 16 stored blocks; slot_rows[a, b, s] is even where b is even and odd where b is odd. `slot_cols`: two stored blocks at the same position add. `reward_cols`: distinct candidates.
All inputs are finite; a program needn't handle non-finite values.
Results may differ from a plain program's by a relative error of at most 0.0003.
Values may be sent and summed in bfloat16 or wider, within the bound.
A program may use at most 64 MiB of HBM per device.

v0:
```python
import jax
import jax.numpy as jnp
from jax import lax
from jax.sharding import PartitionSpec as P

BLK = 128
REWARDS = 16
GROUP = 32


def apply_slots(
    stored,
    rows_here,
    cols_here,
    live_count,
    reward_cells,
    weight_cells,
    value_acc,
    grad_acc,
    passes_mode,
):
    group_count = (live_count + GROUP - 1) // GROUP

    def visit(group_index, totals):
        value_now, grad_now = totals
        first_slot = group_index * GROUP
        block_set = lax.dynamic_slice_in_dim(stored, first_slot, GROUP, 0)
        row_set = lax.dynamic_slice_in_dim(rows_here, first_slot, GROUP, 0)
        col_set = lax.dynamic_slice_in_dim(cols_here, first_slot, GROUP, 0)
        live_mask = (first_slot + jnp.arange(GROUP, dtype=jnp.int32) < live_count).astype(
            jnp.float32
        )[None, :, None]
        if passes_mode != "adjoint":
            picked = jnp.take(reward_cells, col_set, axis=1)
            product = jnp.einsum(
                "kgc,grc->kgr", picked, block_set, preferred_element_type=jnp.float32
            )
            value_now = value_now.at[:, row_set].add(product * live_mask)
        if passes_mode != "forward":
            weights = jnp.take(weight_cells, row_set, axis=1)
            product = jnp.einsum(
                "kgr,grc->kgc", weights, block_set, preferred_element_type=jnp.float32
            )
            grad_now = grad_now.at[:, col_set].add(product * live_mask)
        return (value_now, grad_now)

    return lax.fori_loop(0, group_count, visit, (value_acc, grad_acc))


def on_device(blocks, slot_rows, slot_cols, counts, reward_table, reward_cols, cotangent):
    stored = blocks[0, 0]
    rows_here = slot_rows[0, 0]
    cols_here = slot_cols[0, 0]
    live_count = counts[0, 0]
    reward_full = lax.all_gather(reward_table, "row", axis=0, tiled=True)
    rewards = jnp.take(reward_full, reward_cols, axis=0)
    sb_col = rewards.shape[1] // BLK
    reward_cells = rewards.reshape(REWARDS, sb_col, BLK)
    weight_full = lax.all_gather(cotangent, "col", axis=1, tiled=True)
    sb_row = weight_full.shape[1] // BLK
    weight_cells = weight_full.reshape(REWARDS, sb_row, BLK)
    value_acc = jnp.zeros((REWARDS, sb_row, BLK), jnp.float32)
    grad_acc = jnp.zeros((REWARDS, sb_col, BLK), jnp.float32)
    value_acc, grad_acc = apply_slots(
        stored,
        rows_here,
        cols_here,
        live_count,
        reward_cells,
        weight_cells,
        value_acc,
        grad_acc,
        "forward",
    )
    value = lax.psum_scatter(
        value_acc.reshape(REWARDS, sb_row * BLK), "col", scatter_dimension=1, tiled=True
    )
    value_acc, grad_acc = apply_slots(
        stored,
        rows_here,
        cols_here,
        live_count,
        reward_cells,
        weight_cells,
        value_acc,
        grad_acc,
        "adjoint",
    )
    grad = lax.psum_scatter(
        grad_acc.reshape(REWARDS, sb_col * BLK), "row", scatter_dimension=0, tiled=True
    )
    return (value, grad)


def solution(mesh):
    placed = (
        P("row", "col", None, None, None),
        P("row", "col", None),
        P("row", "col", None),
        P("row", "col"),
        P("row", "col"),
        P(),
        P(None, ("row", "col")),
    )
    return jax.shard_map(
        on_device,
        mesh=mesh,
        in_specs=placed,
        out_specs=(P(None, ("row", "col")), P("row", "col")),
        check_vma=False,
    )
```

profile of v0, /device:TPU:1, one launch (start us, length us, event | category | flops | bytes accessed | tf_op | source)
XLA Modules:
  0.0 299.1 jit_solution(17818313954906341521)
XLA Ops:
  7.2 0.7 all-gather.3.cloned.1.call-update
  9.3 0.7 compare_and_fusion.2
  9.9 24.2 %all-gather = bf16[8,4,8192]{2,1,0:T(4,128)(2,1)S(1)} all-gather(bf16[1,4,8192]{2,1,0:T(4,128)(2,1)} %bitcast.46), channel_id=1, replica_groups=mesh['row'=8,'col'=32] {'row'}, dimensions={0}, use_global_device_ids=true | all-gather | bytes 589824 | tf_op jit(solution)/shard_map/all_gather | solution.py:55
  34.3 0.7 gather_fusion.2
  35.3 25.4 %while.20 = (s32[]{:T(128)}, f32[16,256,128]{2,0,1:T(8,128)S(1)}, s32[]{:T(128)}, s32[256]{0:T(256)S(1)}, bf16[256,128,128]{2,1,0:T(8,128)(2,1)}, /*index=5*/s32...) while((s32[]{:T(128)}, f32[16,256,128]{2,0,1:T(8,128)S(1)}, ...), condition=%wide.region_2.3_spmd, body=%wide.region_0.0_spmd.sunk | while | flops 16975236 | bytes 2495863 | solution.py:47
  35.3 0.7 compare_and_fusion.5
  36.6 1.9 fusion.28
  38.7 1.7 scatter_fusion
  40.4 0.7 compare_and_fusion.5
  41.7 1.9 fusion.28
  43.7 1.7 scatter_fusion
  45.5 0.7 compare_and_fusion.5
  46.8 1.9 fusion.28
  48.8 1.7 scatter_fusion
  50.5 0.7 compare_and_fusion.5
  51.8 1.9 fusion.28
  53.9 1.7 scatter_fusion
  55.6 0.7 compare_and_fusion.5
  56.9 1.9 fusion.28
  58.9 1.7 scatter_fusion
  60.7 2.0 all-gather.3.cloned.1.call-done
  62.7 2.4 copy_bitcast_fusion.1
  65.1 30.2 %while.21 = (s32[]{:T(128)}, f32[16,64,128]{2,0,1:T(8,128)S(1)}, s32[]{:T(128)}, s32[256]{0:T(256)S(1)}, bf16[256,128,128]{2,1,0:T(8,128)(2,1)}, /*index=5*/s32[...) while((s32[]{:T(128)}, f32[16,64,128]{2,0,1:T(8,128)S(1)}, ...), condition=%wide.region_6.7_spmd, body=%wide.region_4.6_spmd.sunk | while | flops 16975236 | bytes 2495863 | solution.py:47
  65.1 0.7 compare_and_fusion.6
  65.9 1.8 gather_fusion.1
  67.7 1.7 fusion.31
  69.4 1.7 scatter_fusion.1
  71.2 0.7 compare_and_fusion.6
  71.9 1.8 gather_fusion.1
  73.7 1.7 fusion.31
  75.5 1.7 scatter_fusion.1
  77.2 0.7 compare_and_fusion.6
  78.0 1.8 gather_fusion.1
  79.8 1.7 fusion.31
  81.5 1.7 scatter_fusion.1
  83.3 0.7 compare_and_fusion.6
  84.0 1.8 gather_fusion.1
  85.8 1.7 fusion.31
  87.6 1.7 scatter_fusion.1
  89.3 0.7 compare_and_fusion.6
  90.1 1.8 gather_fusion.1
  91.9 1.7 fusion.31
  93.6 1.7 scatter_fusion.1
  95.3 0.8 copy_bitcast_fusion.2
  96.3 1.5 copy_bitcast_fusion
  99.6 100.2 %all-reduce.3.cloned.1.call-done = f32[16,8192]{1,0:T(8,128)} async-done(((f32[16,8192]{1,0:T(8,128)}), f32[16,8192]{1,0:T(8,128)}) %all-reduce.3.cloned.1.call-update) | async-done | bytes 524304
  199.9 1.6 constant_dynamic-slice_fusion
  201.5 91.1 %reduce-scatter.2.cloned.1.call-done = f32[16,1024]{1,0:T(8,128)} async-done(((f32[16,32768]{1,0:T(8,128)}), f32[16,1024]{1,0:T(8,128)}) %reduce-scatter.2.cloned.1.call-update) | async-done | bytes 65552 | tf_op jit(solution)/shard_map/reduce_scatter | solution.py:75
  (43 shorter events, 6.3 us)
Async XLA Ops:
  7.2 55.5 %all-gather.3.cloned.1.call-start = ((), (), s32[]{:S(2)}) async-start(), calls=%async_computation.2 | async-start | bytes 1081344 | tf_op jit(solution)/shard_map/all_gather | solution.py:59
  7.9 192.0 %all-reduce.3.cloned.1.call-start = ((), (), s32[]{:S(2)}) async-start(), calls=%async_computation.3 | async-start | bytes 1048576
  34.3 1.0 copy-start
  34.3 1.0 copy-start.1
  96.2 196.4 %reduce-scatter.2.cloned.1.call-start = ((), (), s32[]{:S(2)}) async-start(), calls=%async_computation.1 | async-start | bytes 2162688 | tf_op jit(solution)/shard_map/reduce_scatter | solution.py:75
  97.7 0.7 copy-start.2
Sparse Core Ops, SparseCore 0:
  10.6 52.0 all-gather.2
  96.3 103.5 all-reduce.2
  204.8 87.7 reduce-scatter.1
where the time goes:
time: 301 us; the launch traced here: 299 us
  waiting for transfers between devices  194 us (64%)
  other arithmetic  26.7 us (9%)
  blocking collectives  24.2 us (8%)
  local copies, waits for them, and re-layouts  20.6 us (7%)
  matrix products  17.9 us (6%)
  between operations  15.2 us (5%)
    unnamed x4, waiting for transfers between devices  101 us
    reduce_scatter x1, waiting for transfers between devices, on_device(): lax.psum_scatter(value_acc.reshape(REWARDS, sb_row * BLK), 'col', scatter...  91.1 us
    all_gather x1, blocking collectives, on_device(): reward_full = lax.all_gather(reward_table, 'row', axis=0, tiled=True)  24.2 us
    dot_general x5, matrix products, visit(): jnp.einsum('kgc,grc->kgr', picked, block_set, preferred_element_type=jnp....  9.6 us
    gather x5, local copies, waits for them, and re-layouts, visit(): weights = jnp.take(weight_cells, row_set, axis=1)  9.09 us
    scatter-add x5, other arithmetic, visit(): grad_now = grad_now.at[:, col_set].add(product * live_mask)  8.55 us
    scatter-add x5, other arithmetic, visit(): value_now = value_now.at[:, row_set].add(product * live_mask)  8.51 us
    dot_general x5, matrix products, visit(): jnp.einsum('kgr,grc->kgc', weights, block_set, preferred_element_type=jnp...  8.33 us
  transfers between devices with their start and end apart: 3, of which 3 were waited for; matrix products, arithmetic and copies ran while one was open for 10% of the time, Pallas kernels for 0%

commit v1 on v0

v1 whole, which is shorter than its diff:
```python
import functools

import jax
import jax.numpy as jnp
from jax import lax
from jax.experimental import pallas as pl
from jax.experimental.pallas import tpu as pltpu
from jax.sharding import PartitionSpec as P

F32 = jnp.float32
BF16 = jnp.bfloat16
MESH = pl.DeviceIdType.MESH
NT = (((1,), (1,)), ((), ()))
NZ = 8
NX = 4
NY = 4
VMEM_BYTES = 48 << 20
UNROLL = 32
CHUNKS = 8


def position():
    z = lax.axis_index("row")
    col = lax.axis_index("col")
    return z, lax.rem(lax.div(col, 2), NX), lax.div(col, 2 * NX), lax.rem(col, 2)


def device(z, x, y, core):
    return (z, (y * NX + x) * 2 + core)


def plane_peers(z, x, y, core):
    peers = [device(z, x, y, 1 - core)]
    for i in range(1, NX):
        for c in range(2):
            peers.append(device(z, lax.rem(x + i, NX), y, c))
            peers.append(device(z, x, lax.rem(y + i, NY), c))
    return peers


def barrier(peers):
    semaphore = pltpu.get_barrier_semaphore()
    for peer in peers:
        pl.semaphore_signal(semaphore, inc=1, device_id=peer, device_id_type=MESH)
    pl.semaphore_wait(semaphore, len(peers))


def remote(src, dst, send, recv, peer):
    return pltpu.make_async_remote_copy(
        src_ref=src, dst_ref=dst, send_sem=send, recv_sem=recv, device_id=peer, device_id_type=MESH
    )


def gather_kernel(
    table, cols, cot, rew_out, w_out,
    tab, tabf, own_cot, full, sel, w, cols_s,
    load_sem, zsend, zrecv, psend, precv, qsend, qrecv,
):
    z, x, y, core = position()
    chip = y * NX + x
    loads = [
        pltpu.make_async_copy(table, tab, load_sem.at[0]),
        pltpu.make_async_copy(cols, cols_s, load_sem.at[1]),
    ]
    for t in range(8):
        loads.append(
            pltpu.make_async_copy(
                cot.at[:, pl.ds(t * 128, 128)], own_cot.at[t % 2, t // 2], load_sem.at[2 + t]
            )
        )
    for load in loads:
        load.start()
    up = device(lax.rem(z + 1, NZ), x, y, core)
    down = device(lax.rem(z + NZ - 1, NZ), x, y, core)
    semaphore = pltpu.get_barrier_semaphore()
    peers = [up, down] + plane_peers(z, x, y, core)
    for peer in peers:
        pl.semaphore_signal(semaphore, inc=1, device_id=peer, device_id_type=MESH)
    loads[0].wait()
    for j in range(64):
        tabf[pl.ds(j, 4, stride=64), :] = tab[:, j * 128 : (j + 1) * 128].astype(F32)
    for r in range(4):
        full[z * 4 + r] = tabf[r * 64 : (r + 1) * 64].astype(BF16)
    pl.semaphore_wait(semaphore, len(peers))

    def hop(d, r, way):
        back = lax.rem(z + NZ - (d - 1), NZ) if way == 0 else lax.rem(z + d - 1, NZ)
        piece = full.at[back * 4 + r]
        at = (way, d - 1, r)
        return remote(piece, piece, zsend.at[at], zrecv.at[at], up if way == 0 else down)

    def arrived(d, r, way):
        origin = lax.rem(z + NZ - d, NZ) if way == 0 else lax.rem(z + d, NZ)
        piece = full.at[origin * 4 + r]
        at = (way, d - 1, r)
        return remote(piece, piece, zsend.at[at], zrecv.at[at], up if way == 0 else down)

    def ways(d, r):
        return (0, 1) if d < 4 else ((0,) if r < 2 else (1,))

    for r in range(4):
        for way in ways(1, r):
            hop(1, r, way).start()
    for load in loads[2:]:
        load.wait()

    first = []
    for i in range(NX):
        tx = lax.rem(x + i * (1 - core), NX)
        ty = lax.rem(y + i * core, NY)
        for c in range(2):
            if i == 0:
                if c == 0:
                    first.append(
                        remote(
                            own_cot.at[1 - core], w.at[y, x, core],
                            psend.at[0, 0], precv.at[core, 0], device(z, x, y, 1 - core),
                        )
                    )
                continue
            first.append(
                remote(
                    own_cot.at[c], w.at[y, x, core],
                    psend.at[i, c], precv.at[core, i], device(z, tx, ty, c),
                )
            )
    for copy in first:
        copy.start()
    mine = pltpu.make_async_copy(own_cot.at[core], w.at[y, x, core], load_sem.at[1])
    loads[1].wait()
    mine.start()

    for r in range(4):
        for way in ways(1, r):
            arrived(1, r, way).wait_recv()
            if way in ways(2, r):
                hop(2, r, way).start()

    def first_arrived(i, half):
        piece = w.at[lax.rem(y + NY - i * half, NY), lax.rem(x + NX - i * (1 - half), NX), half]
        return remote(own_cot.at[0], piece, psend.at[0, 0], precv.at[half, i], device(z, x, y, 1 - core))

    mine.wait()
    remote(
        own_cot.at[0], w.at[y, x, 1 - core], psend.at[0, 0], precv.at[1 - core, 0], device(z, x, y, 1 - core)
    ).wait_recv()
    for i in range(1, NX):
        for half in range(2):
            first_arrived(i, half).wait_recv()

    second = []
    for i in range(1, NX):
        second.append(
            remote(
                w.at[y, :, 0], w.at[y, :, 0], qsend.at[0, i], qrecv.at[0, i],
                device(z, x, lax.rem(y + i, NY), core),
            )
        )
        second.append(
            remote(
                w.at[:, x, 1], w.at[:, x, 1], qsend.at[1, i], qrecv.at[1, i],
                device(z, lax.rem(x + i, NX), y, core),
            )
        )
    for copy in second:
        copy.start()

    for d in (2, 3):
        for r in range(4):
            for way in ways(d, r):
                arrived(d, r, way).wait_recv()
                if way in ways(d + 1, r):
                    hop(d + 1, r, way).start()
    for i in range(1, NX):
        sy = lax.rem(y + NY - i, NY)
        sx = lax.rem(x + NX - i, NX)
        remote(w.at[sy, :, 0], w.at[sy, :, 0], qsend.at[0, i], qrecv.at[0, i], up).wait_recv()
        remote(w.at[:, sx, 1], w.at[:, sx, 1], qsend.at[1, i], qrecv.at[1, i], up).wait_recv()
    w_out[...] = w[...].reshape(w_out.shape)
    for r in range(4):
        for way in ways(4, r):
            arrived(4, r, way).wait_recv()
    for k in range(16):
        sel[k * 64 : (k + 1) * 64] = full[cols_s[k]].astype(F32)
    for j in range(64):
        rew_out[j] = sel[pl.ds(j, 16, stride=64), :].astype(BF16)
    for d in (1, 2, 3, 4):
        for r in range(4):
            for way in ways(d, r):
                hop(d, r, way).wait_send()
    for copy in first + second:
        copy.wait_send()


def gather(table, cols, cot):
    anywhere = pl.BlockSpec(memory_space=pl.ANY)
    vmem = pl.BlockSpec(memory_space=pltpu.VMEM)
    dma = pltpu.SemaphoreType.DMA
    return pl.pallas_call(
        gather_kernel,
        out_shape=(
            jax.ShapeDtypeStruct((64, 16, 128), BF16),
            jax.ShapeDtypeStruct((128, 16, 128), BF16),
        ),
        in_specs=[anywhere] * 3,
        out_specs=(vmem, vmem),
        scratch_shapes=[
            pltpu.VMEM((4, 8192), BF16),
            pltpu.VMEM((256, 128), F32),
            pltpu.VMEM((2, 4, 16, 128), BF16),
            pltpu.VMEM((32, 64, 128), BF16),
            pltpu.VMEM((1024, 128), F32),
            pltpu.VMEM((NY, NX, 2, 4, 16, 128), BF16),
            pltpu.SMEM((16,), jnp.int32),
            dma((10,)),
            dma((2, 4, 4)),
            dma((2, 4, 4)),
            dma((4, 2)),
            dma((2, 4)),
            dma((2, 4)),
            dma((2, 4)),
        ],
        compiler_params=pltpu.CompilerParams(
            collective_id=0, has_side_effects=True, vmem_limit_bytes=VMEM_BYTES
        ),
    )(table, cols, cot)


def product_kernel(
    slot_rows, slot_cols, counts, blocks, rew, w, val, grad_rows,
    rows_s, cols_s, count_s, stored, grad, sem,
):
    each = 256 // CHUNKS
    small = [
        pltpu.make_async_copy(slot_rows, rows_s, sem.at[CHUNKS]),
        pltpu.make_async_copy(slot_cols, cols_s, sem.at[CHUNKS + 1]),
        pltpu.make_async_copy(counts, count_s, sem.at[CHUNKS + 2]),
    ]
    large = [
        pltpu.make_async_copy(
            blocks.at[0, 0, pl.ds(i * each, each)], stored.at[pl.ds(i * each, each)], sem.at[i]
        )
        for i in range(CHUNKS)
    ]
    for copy in small + large:
        copy.start()
    val[...] = jnp.zeros_like(val)
    grad[...] = jnp.zeros_like(grad)
    for copy in small:
        copy.wait()
    live = count_s[0, 0]
    zero = jnp.zeros((16, 128), BF16)
    for i in range(CHUNKS):
        large[i].wait()

        @pl.loop(i * each, (i + 1) * each, step=UNROLL)
        def _(start):
            places, forward, adjoint = [], [], []
            for u in range(0, UNROLL, 2):
                s = start + u
                pair = stored[pl.ds(s, 2)].reshape(256, 128)
                r0, r1 = lax.div(rows_s[0, 0, s], 2), lax.div(rows_s[0, 0, s + 1], 2)
                c0, c1 = cols_s[0, 0, s], cols_s[0, 0, s + 1]
                m0, m1 = (s < live).astype(F32), (s + 1 < live).astype(F32)
                left = jnp.concatenate([rew[c0], rew[c1]], axis=0)
                out = lax.dot_general(left, pair, NT, preferred_element_type=F32)
                forward += [out[:16, :128] * m0, out[16:, 128:] * m1]
                left = jnp.concatenate(
                    [
                        jnp.concatenate([w[r0], zero], axis=1),
                        jnp.concatenate([zero, w[r1]], axis=1),
                    ],
                    axis=0,
                )
                out = jnp.dot(left, pair, preferred_element_type=F32)
                adjoint += [out[:16] * m0, out[16:] * m1]
                places += [(r0, c0), (r1, c1)]
            for u, (r, c) in enumerate(places):
                val[r] += forward[u]
                grad[pl.ds(c * 16, 16)] += adjoint[u]

    for k in range(16):
        grad_rows[k] = grad[pl.ds(k, 64, stride=16), :]


def products(slot_rows, slot_cols, counts, blocks, rew, w):
    anywhere = pl.BlockSpec(memory_space=pl.ANY)
    vmem = pl.BlockSpec(memory_space=pltpu.VMEM)
    return pl.pallas_call(
        product_kernel,
        out_shape=(
            jax.ShapeDtypeStruct((128, 16, 128), F32),
            jax.ShapeDtypeStruct((16, 64, 128), F32),
        ),
        in_specs=[anywhere] * 4 + [vmem] * 2,
        out_specs=(vmem, vmem),
        scratch_shapes=[
            pltpu.SMEM((1, 1, 256), jnp.int32),
            pltpu.SMEM((1, 1, 256), jnp.int32),
            pltpu.SMEM((1, 1), jnp.int32),
            pltpu.VMEM((256, 128, 128), BF16),
            pltpu.VMEM((1024, 128), F32),
            pltpu.SemaphoreType.DMA((CHUNKS + 3,)),
        ],
        compiler_params=pltpu.CompilerParams(vmem_limit_bytes=VMEM_BYTES),
    )(slot_rows, slot_cols, counts, blocks, rew, w)


def scatter_kernel(
    val, grad_rows, value_out, grad_out,
    zbuf, zin, abuf, bbuf, asum, bsum, fin, gsum,
    zsend, zrecv, psend, precv, qsend, qrecv,
):
    z, x, y, core = position()
    up = device(lax.rem(z + 1, NZ), x, y, core)
    down = device(lax.rem(z + NZ - 1, NZ), x, y, core)
    barrier([up, down] + plane_peers(z, x, y, core))

    def owner(way, d):
        return lax.rem(z + d, NZ) if way == 0 else lax.rem(z + NZ - d, NZ)

    def send(way, d, r, first):
        at = (way, d - 1, r)
        src = grad_rows.at[owner(way, d) * 2 + r] if first else zbuf.at[at]
        return remote(src, zin.at[at], zsend.at[at], zrecv.at[at], up if way == 0 else down)

    far = {(0, 0): 4, (0, 1): 3, (1, 0): 3, (1, 1): 4}
    for r in (0, 1):
        for way in (0, 1):
            send(way, far[way, r], r, True).start()

    first = []
    for i in range(1, NX):
        tx = lax.rem(x + i, NX)
        ty = lax.rem(y + i, NY)
        first.append(
            remote(val.at[:, tx, 0], abuf.at[i - 1], psend.at[0, i - 1], precv.at[0, i - 1], device(z, tx, y, core))
        )
        first.append(
            remote(val.at[ty, :, 1], bbuf.at[i - 1], psend.at[1, i - 1], precv.at[1, i - 1], device(z, x, ty, core))
        )
    for copy in first:
        copy.start()

    def relay(d):
        for way in (0, 1):
            for r in (0, 1):
                if d + 1 > far[way, r]:
                    continue
                send(way, d + 1, r, False).wait_recv()
                at = (way, d - 1, r)
                zbuf[at] = zin[way, d, r] + grad_rows[owner(way, d) * 2 + r]
                send(way, d, r, False).start()

    relay(3)
    relay(2)
    for copy in first:
        copy.wait_recv()
    asum[...] = val[:, x, 0] + abuf[0] + abuf[1] + abuf[2]
    bsum[...] = val[y, :, 1] + bbuf[0] + bbuf[1] + bbuf[2]

    second = []
    for i in range(1, NX):
        ty = lax.rem(y + i, NY)
        tx = lax.rem(x + i, NX)
        second.append(
            remote(asum.at[ty], fin.at[core, i], qsend.at[0, i], qrecv.at[core, i], device(z, x, ty, 0))
        )
        second.append(
            remote(bsum.at[tx], fin.at[core, i], qsend.at[1, i], qrecv.at[core, i], device(z, tx, y, 1))
        )
    for copy in second:
        copy.start()
    partner = device(z, x, y, 1 - core)

    @pl.when(core == 0)
    def _():
        remote(bsum.at[x], fin.at[core, 0], qsend.at[0, 0], qrecv.at[core, 0], partner).start()
        fin[core, 0] = asum[y]

    @pl.when(core == 1)
    def _():
        remote(asum.at[y], fin.at[core, 0], qsend.at[0, 0], qrecv.at[core, 0], partner).start()
        fin[core, 0] = bsum[x]

    relay(1)
    last = remote(asum.at[0], fin.at[1 - core, 0], qsend.at[0, 0], qrecv.at[1 - core, 0], partner)
    last.wait_recv()
    for c in range(2):
        for i in range(1, NX):
            remote(asum.at[0], fin.at[c, i], qsend.at[0, i], qrecv.at[c, i], partner).wait_recv()
    for t in range(8):
        p, h = t % 2, t // 2
        value_out[:, t * 128 : (t + 1) * 128] = fin[p, 0, h] + fin[p, 1, h] + fin[p, 2, h] + fin[p, 3, h]
    for way in (0, 1):
        for r in (0, 1):
            send(way, 1, r, False).wait_recv()
    for r in (0, 1):
        gsum[r * 64 : (r + 1) * 64] = grad_rows[z * 2 + r] + zin[0, 0, r] + zin[1, 0, r]
    for j in range(64):
        grad_out[:, j * 128 : (j + 1) * 128] = gsum[pl.ds(j, 2, stride=64), :]
    for way in (0, 1):
        for r in (0, 1):
            for d in range(1, far[way, r] + 1):
                send(way, d, r, d == far[way, r]).wait_send()
    for copy in first + second:
        copy.wait_send()
    last.wait_send()


def scatter(val, grad_rows):
    vmem = pl.BlockSpec(memory_space=pltpu.VMEM)
    dma = pltpu.SemaphoreType.DMA
    return pl.pallas_call(
        scatter_kernel,
        out_shape=(jax.ShapeDtypeStruct((16, 1024), F32), jax.ShapeDtypeStruct((2, 8192), F32)),
        in_specs=[vmem, vmem],
        out_specs=(vmem, vmem),
        scratch_shapes=[
            pltpu.VMEM((2, 4, 2, 64, 128), F32),
            pltpu.VMEM((2, 4, 2, 64, 128), F32),
            pltpu.VMEM((3, 4, 4, 16, 128), F32),
            pltpu.VMEM((3, 4, 4, 16, 128), F32),
            pltpu.VMEM((4, 4, 16, 128), F32),
            pltpu.VMEM((4, 4, 16, 128), F32),
            pltpu.VMEM((2, 4, 4, 16, 128), F32),
            pltpu.VMEM((128, 128), F32),
            dma((2, 4, 2)),
            dma((2, 4, 2)),
            dma((2, 3)),
            dma((2, 3)),
            dma((2, 4)),
            dma((2, 4)),
        ],
        compiler_params=pltpu.CompilerParams(
            collective_id=1, has_side_effects=True, vmem_limit_bytes=VMEM_BYTES
        ),
    )(val, grad_rows)


def on_device(blocks, slot_rows, slot_cols, counts, reward_table, reward_cols, cotangent):
    rew, w = gather(reward_table, reward_cols, cotangent)
    val, grad_rows = products(slot_rows, slot_cols, counts, blocks, rew, w)
    return scatter(val.reshape(NY, NX, 2, 4, 16, 128), grad_rows)


def solution(mesh):
    placed = (
        P("row", "col", None, None, None),
        P("row", "col", None),
        P("row", "col", None),
        P("row", "col"),
        P("row", "col"),
        P(),
        P(None, ("row", "col")),
    )
    return jax.shard_map(
        on_device,
        mesh=mesh,
        in_specs=placed,
        out_specs=(P(None, ("row", "col")), P("row", "col")),
        check_vma=False,
    )
```

time: 301 us -> 51.8 us (0.17)
  waiting for transfers between devices: 194 us -> 0 us
  Pallas kernels: 0 us -> 45.1 us
  other arithmetic: 26.7 us -> 0 us
  blocking collectives: 24.2 us -> 0 us
  matrix products: 17.9 us -> 0 us
  local copies, waits for them, and re-layouts: 20.6 us -> 4.86 us
  between operations: 15.2 us -> 1.32 us
    unnamed x4 -> x0, waiting for transfers between devices: 101 us -> none
    reduce_scatter x1 -> x0, waiting for transfers between devices: 91.1 us -> none  [on_device(): lax.psum_scatter(value_acc.reshape(REWARDS, sb_row * BLK), 'col', scatter...]
    pallas_call x0 -> x3, Pallas kernels: none -> 45.1 us  [the longest x1 20.5 us: gather(): pl.pallas_call(gather_kernel, out_shape=(jax.ShapeDtypeStruct((64, 16, 12...]
    all_gather x1 -> x0, blocking collectives: 24.2 us -> none  [on_device(): reward_full = lax.all_gather(reward_table, 'row', axis=0, tiled=True)]
    dot_general x10 -> x0, matrix products: 17.9 us -> none  [the longest x5 9.6 us: visit(): jnp.einsum('kgc,grc->kgr', picked, block_set, preferred_element_type=jnp....]
    scatter-add x10 -> x0, other arithmetic: 17.1 us -> none  [the longest x5 8.55 us: visit(): grad_now = grad_now.at[:, col_set].add(product * live_mask)]
    gather x11 -> x0, local copies, waits for them, and re-layouts: 12.8 us -> none  [the longest x5 9.09 us: visit(): weights = jnp.take(weight_cells, row_set, axis=1)]
    and x11 -> x0, other arithmetic: 7.94 us -> none  [the longest x5 3.64 us: visit(): picked = jnp.take(reward_cells, col_set, axis=1)]
  transfers between devices with their start and end apart: 3 -> 0, of which waited for: 3 -> 0; matrix products, arithmetic and copies ran while one was open for 10% -> 0% of each run, Pallas kernels for 0% -> 0%
where the time goes in v1:
time: 51.8 us; the launch traced here: 51.3 us
  Pallas kernels  45.1 us (87%)
  local copies, waits for them, and re-layouts  4.86 us (9%)
  between operations  1.32 us (3%)
    pallas_call x1, Pallas kernels, gather(): pl.pallas_call(gather_kernel, out_shape=(jax.ShapeDtypeStruct((64, 16, 12...  20.5 us
    pallas_call x1, Pallas kernels, scatter(): pl.pallas_call(scatter_kernel, out_shape=(jax.ShapeDtypeStruct((16, 1024)...  18.6 us
    pallas_call x1, Pallas kernels, products(): pl.pallas_call(product_kernel, out_shape=(jax.ShapeDtypeStruct((128, 16,...  6.04 us
    unnamed x12, local copies, waits for them, and re-layouts  4.86 us

profile of v1, /device:TPU:1, one launch (start us, length us, event | category | flops | bytes accessed | tf_op | source)
XLA Modules:
  0.0 51.3 jit_solution(26793844593453398)
XLA Ops:
  1.3 0.0 copy-start
  1.3 0.8 %copy-done = bf16[4,8192]{1,0:T(4,128)(2,1)S(1)} copy-done((bf16[4,8192]{1,0:T(4,128)(2,1)S(1)}, bf16[4,8192]{1,0:T(4,128)(2,1)}, u32[]{:S(2)}) %copy-start) | copy-done | bytes 65560
  2.1 0.0 copy-start.1
  2.1 0.8 %copy-done.1 = bf16[16,1024]{1,0:T(8,128)(2,1)S(1)} copy-done((bf16[16,1024]{1,0:T(8,128)(2,1)S(1)}, bf16[16,1024]{1,0:T(8,128)(2,1)}, u32[]{:S(2)}) %copy-start.1) | copy-done | bytes 32792
  2.9 0.0 copy-start.4
  2.9 0.7 %copy-done.4 = s32[16]{0:T(128)S(1)} copy-done((s32[16]{0:T(128)S(1)}, s32[16]{0:T(128)}, u32[]{:S(2)}) %copy-start.4) | copy-done | bytes 88
  3.5 20.5 %shard_map.86 = (bf16[64,16,128]{2,1,0:T(8,128)(2,1)S(1)}, bf16[128,16,128]{2,1,0:T(8,128)(2,1)S(1)}) custom-call(bf16[4,8192]{1,0:T(4,128)(2,1)S(1)} %copy-done, s32[16]{0:T(128)S(1)} %copy-done.4, bf16[16,1024]{1,0:T(8,128)(2,1)S(1)} %copy-done.1), custom_call_target="tpu_custom_call" | custom-call | tf_op jit(solution)/shard_map/pallas_call | solution.py:199
  24.0 0.0 copy-start.2
  24.0 0.7 %copy-done.2 = s32[1,1,256]{2,1,0:T(1,128)S(1)} copy-done((s32[1,1,256]{2,1,0:T(1,128)S(1)}, s32[1,1,256]{2,1,0:T(1,128)}, u32[]{:S(2)}) %copy-start.2) | copy-done | bytes 1048
  24.7 0.0 copy-start.3
  24.7 0.7 %copy-done.3 = s32[1,1,256]{2,1,0:T(1,128)S(1)} copy-done((s32[1,1,256]{2,1,0:T(1,128)S(1)}, s32[1,1,256]{2,1,0:T(1,128)}, u32[]{:S(2)}) %copy-start.3) | copy-done | bytes 1048
  25.4 6.0 %shard_map.87 = (f32[128,16,128]{2,1,0:T(8,128)S(1)}, f32[16,64,128]{2,1,0:T(8,128)S(1)}) custom-call(s32[1,1,256]{2,1,0:T(1,128)S(1)} %copy-done.2, s32[1,1,256]{2,1,0:T(1,128)S(1)} %copy-done.3, s32[1,1]{1,0:T(1,128)S(6)} %copy.11.counts, bf16[1,1,256,128,128]{4,3,2,1,0:T(8,128)(2,1)} %blocks.1, bf16[64,16,128]{2,1,0:T(8,128)(2,1)S(1)} %get-tuple-element.6.rew, ...), custom_call_target="tpu_custom_call" | custom-call | tf_op jit(solution)/shard_map/pallas_call | solution.py:289
  31.4 18.6 %shard_map.88 = (f32[16,1024]{1,0:T(8,128)S(1)}, f32[2,8192]{1,0:T(2,128)S(1)}) custom-call(f32[4,4,2,4,16,128]{5,4,3,2,1,0:T(8,128)S(1)} %bitcast.1, f32[16,64,128]{2,1,0:T(8,128)S(1)} %get-tuple-element.9.grad_rows), custom_call_target="tpu_custom_call" | custom-call | tf_op jit(solution)/shard_map/pallas_call | solution.py:414
  50.0 0.6 %copy.12 = f32[16,1024]{1,0:T(8,128)} copy(f32[16,1024]{1,0:T(8,128)S(1)} %get-tuple-element.12) | data formatting | bytes 131072
  50.7 0.6 %copy.13 = f32[2,8192]{1,0:T(2,128)} copy(f32[2,8192]{1,0:T(2,128)S(1)} %get-tuple-element.13) | data formatting | bytes 131072
Async XLA Ops:
  1.3 0.8 %copy-start = (bf16[4,8192]{1,0:T(4,128)(2,1)S(1)}, bf16[4,8192]{1,0:T(4,128)(2,1)}, u32[]{:S(2)}) copy-start(bf16[4,8192]{1,0:T(4,128)(2,1)} %table.1) | copy-start | bytes 196612
  2.1 0.8 %copy-start.1 = (bf16[16,1024]{1,0:T(8,128)(2,1)S(1)}, bf16[16,1024]{1,0:T(8,128)(2,1)}, u32[]{:S(2)}) copy-start(bf16[16,1024]{1,0:T(8,128)(2,1)} %cot.1) | copy-start | bytes 98308
  2.9 0.7 %copy-start.4 = (s32[16]{0:T(128)S(1)}, s32[16]{0:T(128)}, u32[]{:S(2)}) copy-start(s32[16]{0:T(128)} %cols.1) | copy-start | bytes 196
  24.0 0.7 %copy-start.2 = (s32[1,1,256]{2,1,0:T(1,128)S(1)}, s32[1,1,256]{2,1,0:T(1,128)}, u32[]{:S(2)}) copy-start(s32[1,1,256]{2,1,0:T(1,128)} %slot_rows.1) | copy-start | bytes 3076
  24.7 0.7 %copy-start.3 = (s32[1,1,256]{2,1,0:T(1,128)S(1)}, s32[1,1,256]{2,1,0:T(1,128)}, u32[]{:S(2)}) copy-start(s32[1,1,256]{2,1,0:T(1,128)} %slot_cols.1) | copy-start | bytes 3076

commit v2 on v0

v2 whole, which is shorter than its diff:
```python
import functools

import jax
import jax.numpy as jnp
from jax import lax
from jax.experimental import pallas as pl
from jax.experimental.pallas import tpu as pltpu
from jax.sharding import PartitionSpec as P

F32 = jnp.float32
BF16 = jnp.bfloat16
MESH = pl.DeviceIdType.MESH
NT = (((1,), (1,)), ((), ()))
NZ = 8
NX = 4
NY = 4
VMEM_BYTES = 62 << 20
UNROLL = 64
CHUNKS = 8


def position():
    z = lax.axis_index("row")
    col = lax.axis_index("col")
    return z, lax.rem(lax.div(col, 2), NX), lax.div(col, 2 * NX), lax.rem(col, 2)


def device(z, x, y, core):
    return (z, (y * NX + x) * 2 + core)


def plane_peers(z, x, y, core):
    peers = [device(z, x, y, 1 - core)]
    for i in range(1, NX):
        for c in range(2):
            peers.append(device(z, lax.rem(x + i, NX), y, c))
            peers.append(device(z, x, lax.rem(y + i, NY), c))
    return peers


def remote(src, dst, send, recv, peer):
    return pltpu.make_async_remote_copy(
        src_ref=src, dst_ref=dst, send_sem=send, recv_sem=recv, device_id=peer, device_id_type=MESH
    )


def one_hot(index, height, live, target):
    rows = lax.broadcasted_iota(jnp.int32, (height, 256), 0)
    slots = lax.broadcasted_iota(jnp.int32, (height, 256), 1)
    hit = (target(rows) == index) & (slots < live)
    return jnp.where(hit, 1.0, 0.0).astype(BF16)


def slot_sums(hot, products, k):
    part = products[pl.ds(k, 256, stride=16), :]
    high = part.astype(BF16)
    low = (part - high.astype(F32)).astype(BF16)
    out = jnp.dot(hot, jnp.concatenate([high, low], axis=1), preferred_element_type=F32)
    return out[:, :128] + out[:, 128:]


def kernel(
    blocks, slot_rows, slot_cols, counts, table, reward_cols, cot, value_out, grad_out,
    stored, rows_s, cols_s, count_s, picks_s, rows_v, cols_v,
    tab, tabf, own_cot, full, sel, rew, w, wf, hot_rows, hot_cols,
    adjoint, forward, vsum, vtile, grads, gsum,
    abuf, bbuf, asum, bsum, fin, near, mid, far, relay,
    load_sem, block_sem, gsend, grecv, psend, precv, qsend, qrecv,
    zsend, zrecv, vsend, vrecv, fsend, frecv,
):
    z, x, y, core = position()
    partner = device(z, x, y, 1 - core)

    def along_z(step):
        return device(lax.rem(z + NZ + step, NZ), x, y, core)

    def at_z(step):
        return lax.rem(z + NZ + step, NZ)

    loads = [
        pltpu.make_async_copy(table, tab, load_sem.at[0]),
        pltpu.make_async_copy(reward_cols, picks_s, load_sem.at[1]),
        pltpu.make_async_copy(slot_rows, rows_s, load_sem.at[2]),
        pltpu.make_async_copy(slot_cols, cols_s, load_sem.at[3]),
        pltpu.make_async_copy(counts, count_s, load_sem.at[4]),
        pltpu.make_async_copy(slot_rows, rows_v, load_sem.at[5]),
        pltpu.make_async_copy(slot_cols, cols_v, load_sem.at[6]),
    ]
    cot_loads = [
        pltpu.make_async_copy(cot.at[:, pl.ds(t * 128, 128)], own_cot.at[t % 2, t // 2], load_sem.at[7 + t])
        for t in range(8)
    ]
    each = 256 // CHUNKS
    block_loads = [
        pltpu.make_async_copy(
            blocks.at[0, 0, pl.ds(i * each, each)], stored.at[pl.ds(i * each, each)], block_sem.at[i]
        )
        for i in range(CHUNKS)
    ]
    for load in loads[:1] + cot_loads + loads[1:] + block_loads:
        load.start()
    semaphore = pltpu.get_barrier_semaphore()
    peers = [along_z(2), along_z(-2), along_z(1), along_z(-1)] + plane_peers(z, x, y, core)
    for peer in peers:
        pl.semaphore_signal(semaphore, inc=1, device_id=peer, device_id_type=MESH)
    loads[0].wait()
    for j in range(64):
        tabf[pl.ds(j, 4, stride=64), :] = tab[:, j * 128 : (j + 1) * 128].astype(F32)
    for r in range(4):
        full[z * 4 + r] = tabf[r * 64 : (r + 1) * 64].astype(BF16)
    for load in cot_loads:
        load.wait()
    pl.semaphore_wait(semaphore, len(peers))

    def reward_copy(way, kind, half, receiving):
        sign = 1 if way == 0 else -1
        reach = (1, 2, 1, 2)[kind]
        origin = -sign * ((1, 2, 3, 4)[kind] if receiving else (0, 0, 2, 2)[kind])
        piece = full.at[pl.ds(at_z(origin) * 4 + half * 2, 2)]
        at = (way, kind, half)
        return remote(piece, piece, gsend.at[at], grecv.at[at], along_z(sign * reach))

    for kind in (1, 0):
        for half in (0, 1):
            for way in (0, 1):
                reward_copy(way, kind, half, False).start()

    first = [remote(own_cot.at[1 - core], w.at[y, x, core], psend.at[0, 0], precv.at[core, 0], partner)]
    for i in range(1, NX):
        tx = lax.rem(x + i * (1 - core), NX)
        ty = lax.rem(y + i * core, NY)
        for c in range(2):
            first.append(
                remote(own_cot.at[c], w.at[y, x, core], psend.at[i, c], precv.at[core, i], device(z, tx, ty, c))
            )
    for copy in first:
        copy.start()
    w[y, x, core] = own_cot[core]

    for load in loads[1:]:
        load.wait()
    live = count_s[0, 0]

    def block_row(at):
        half, a, b, t = at >> 6, (at >> 4) & 3, (at >> 2) & 3, at & 3
        tx, ty = jnp.where(half == 0, a, b), jnp.where(half == 0, b, a)
        return ((ty * NX + tx) * 2 + half) * 8 + t * 2 + core

    hot_rows[...] = one_hot(rows_v[0], 128, live, block_row)
    hot_cols[...] = one_hot(cols_v[0], 64, live, lambda at: at)

    remote(own_cot.at[0], w.at[y, x, 1 - core], psend.at[0, 0], precv.at[1 - core, 0], partner).wait_recv()
    for i in range(1, NX):
        for half in range(2):
            piece = w.at[lax.rem(y + NY - i * half, NY), lax.rem(x + NX - i * (1 - half), NX), half]
            remote(own_cot.at[0], piece, psend.at[0, 0], precv.at[half, i], partner).wait_recv()

    second = []
    for i in range(1, NX):
        row, column = w.at[y, :, 0], w.at[:, x, 1]
        second.append(
            remote(row, row, qsend.at[0, i], qrecv.at[0, i], device(z, x, lax.rem(y + i, NY), core))
        )
        second.append(
            remote(column, column, qsend.at[1, i], qrecv.at[1, i], device(z, lax.rem(x + i, NX), y, core))
        )
    for copy in second:
        copy.start()

    for half in (0, 1):
        for way in (0, 1):
            reward_copy(way, 1, half, True).wait_recv()
            reward_copy(way, 2, half, False).start()
            if half == way:
                reward_copy(way, 3, half, False).start()

    for i in range(1, NX):
        row, column = w.at[lax.rem(y + NY - i, NY), :, 0], w.at[:, lax.rem(x + NX - i, NX), 1]
        remote(row, row, qsend.at[0, i], qrecv.at[0, i], partner).wait_recv()
        remote(column, column, qsend.at[1, i], qrecv.at[1, i], partner).wait_recv()
    wf[...] = w[...].reshape(wf.shape)
    for load in block_loads:
        load.wait()

    zero = jnp.zeros((16, 128), BF16)

    @pl.loop(0, 256, step=UNROLL)
    def _(start):
        for u in range(0, UNROLL, 2):
            s = start + u
            pair = stored[pl.ds(s, 2)].reshape(256, 128)
            w0 = wf[lax.div(rows_s[0, 0, s], 2)]
            w1 = wf[lax.div(rows_s[0, 0, s + 1], 2)]
            left = jnp.concatenate(
                [jnp.concatenate([w0, zero], axis=1), jnp.concatenate([zero, w1], axis=1)], axis=0
            )
            adjoint[pl.ds(pl.multiple_of(s * 16, 32), 32), :] = jnp.dot(left, pair, preferred_element_type=F32)

    for k in range(16):
        grads[k] = slot_sums(hot_cols[...], adjoint, k)

    def sign_of(way):
        return 1 if way == 0 else -1

    def far_copy(way):
        s = sign_of(way)
        return remote(
            grads.at[at_z(4) * 2 + way], far.at[way], zsend.at[way, 0], zrecv.at[way, 0], along_z(2 * s)
        )

    def mid_copy(way):
        s = sign_of(way)
        return remote(
            grads.at[pl.ds(at_z(3 * s) * 2, 2)], mid.at[way], zsend.at[way, 1], zrecv.at[way, 1], along_z(s)
        )

    def near_copy(way):
        s = sign_of(way)
        return remote(
            grads.at[pl.ds(at_z(s) * 2, 2)], near.at[0, way], zsend.at[way, 2], zrecv.at[way, 2], along_z(s)
        )

    def relay_copy(way):
        s = sign_of(way)
        return remote(relay.at[way], near.at[1, way], zsend.at[way, 3], zrecv.at[way, 3], along_z(2 * s))

    for copy in (far_copy, mid_copy, near_copy):
        for way in (0, 1):
            copy(way).start()

    for way in (0, 1):
        for half in (0, 1):
            reward_copy(way, 0, half, True).wait_recv()
            reward_copy(way, 2, half, True).wait_recv()
        reward_copy(way, 3, way, True).wait_recv()
    for k in range(16):
        sel[k * 64 : (k + 1) * 64] = full[picks_s[k]].astype(F32)
    for j in range(64):
        rew[j] = sel[pl.ds(j, 16, stride=64), :].astype(BF16)

    @pl.loop(0, 256, step=UNROLL)
    def _(start):
        for u in range(0, UNROLL, 2):
            s = start + u
            pair = stored[pl.ds(s, 2)].reshape(256, 128)
            left = jnp.concatenate([rew[cols_s[0, 0, s]], rew[cols_s[0, 0, s + 1]]], axis=0)
            out = lax.dot_general(left, pair, NT, preferred_element_type=F32)
            at = pl.multiple_of(s * 16, 32)
            forward[pl.ds(at, 16), :] = out[:16, :128]
            forward[pl.ds(at + 16, 16), :] = out[16:, 128:]

    for k in range(16):
        vsum[k * 128 : (k + 1) * 128] = slot_sums(hot_rows[...], forward, k)
    for i in range(128):
        vtile[i >> 6, (i >> 4) & 3, (i >> 2) & 3, i & 3] = vsum[pl.ds(i, 16, stride=128), :]

    value_first = []
    for i in range(1, NX):
        tx = lax.rem(x + i, NX)
        ty = lax.rem(y + i, NY)
        value_first.append(
            remote(vtile.at[0, tx], abuf.at[i - 1], vsend.at[0, i - 1], vrecv.at[0, i - 1], device(z, tx, y, core))
        )
        value_first.append(
            remote(vtile.at[1, ty], bbuf.at[i - 1], vsend.at[1, i - 1], vrecv.at[1, i - 1], device(z, x, ty, core))
        )
    for copy in value_first:
        copy.start()

    for way in (0, 1):
        mid_copy(way).wait_recv()
        far_copy(way).wait_recv()
        s = sign_of(way)
        relay[way] = grads[pl.ds(at_z(2 * s) * 2, 2)] + mid[way]
        relay[way, way] = relay[way, way] + far[way]
        relay_copy(way).start()

    for copy in value_first:
        copy.wait_recv()
    asum[...] = vtile[0, x] + abuf[0] + abuf[1] + abuf[2]
    bsum[...] = vtile[1, y] + bbuf[0] + bbuf[1] + bbuf[2]

    value_second = []
    for i in range(1, NX):
        ty = lax.rem(y + i, NY)
        tx = lax.rem(x + i, NX)
        value_second.append(
            remote(asum.at[ty], fin.at[core, i], fsend.at[0, i], frecv.at[core, i], device(z, x, ty, 0))
        )
        value_second.append(
            remote(bsum.at[tx], fin.at[core, i], fsend.at[1, i], frecv.at[core, i], device(z, tx, y, 1))
        )
    for copy in value_second:
        copy.start()

    @pl.when(core == 0)
    def _():
        remote(bsum.at[x], fin.at[core, 0], fsend.at[0, 0], frecv.at[core, 0], partner).start()
        fin[core, 0] = asum[y]

    @pl.when(core == 1)
    def _():
        remote(asum.at[y], fin.at[core, 0], fsend.at[0, 0], frecv.at[core, 0], partner).start()
        fin[core, 0] = bsum[x]

    for way in (0, 1):
        near_copy(way).wait_recv()
        relay_copy(way).wait_recv()
    for r in (0, 1):
        gsum[r * 64 : (r + 1) * 64] = (
            grads[z * 2 + r] + near[0, 0, r] + near[0, 1, r] + near[1, 0, r] + near[1, 1, r]
        )
    for j in range(64):
        grad_out[:, j * 128 : (j + 1) * 128] = gsum[pl.ds(j, 2, stride=64), :]

    last = remote(asum.at[0], fin.at[1 - core, 0], fsend.at[0, 0], frecv.at[1 - core, 0], partner)
    last.wait_recv()
    for c in range(2):
        for i in range(1, NX):
            remote(asum.at[0], fin.at[c, i], fsend.at[0, i], frecv.at[c, i], partner).wait_recv()
    for t in range(8):
        p, h = t % 2, t // 2
        value_out[:, t * 128 : (t + 1) * 128] = fin[p, 0, h] + fin[p, 1, h] + fin[p, 2, h] + fin[p, 3, h]

    for way in (0, 1):
        for half in (0, 1):
            for kind in (0, 1, 2):
                reward_copy(way, kind, half, False).wait_send()
        reward_copy(way, 3, way, False).wait_send()
        for copy in (far_copy, mid_copy, near_copy, relay_copy):
            copy(way).wait_send()
    for copy in first + second + value_first + value_second + [last]:
        copy.wait_send()


def on_device(*operands):
    vmem = pl.BlockSpec(memory_space=pltpu.VMEM)
    dma = pltpu.SemaphoreType.DMA
    return pl.pallas_call(
        kernel,
        out_shape=(jax.ShapeDtypeStruct((16, 1024), F32), jax.ShapeDtypeStruct((2, 8192), F32)),
        in_specs=[pl.BlockSpec(memory_space=pltpu.HBM)] * 7,
        out_specs=(vmem, vmem),
        scratch_shapes=[
            pltpu.VMEM((256, 128, 128), BF16),
            pltpu.SMEM((1, 1, 256), jnp.int32),
            pltpu.SMEM((1, 1, 256), jnp.int32),
            pltpu.SMEM((1, 1), jnp.int32),
            pltpu.SMEM((16,), jnp.int32),
            pltpu.VMEM((1, 1, 256), jnp.int32),
            pltpu.VMEM((1, 1, 256), jnp.int32),
            pltpu.VMEM((4, 8192), BF16),
            pltpu.VMEM((256, 128), F32),
            pltpu.VMEM((2, 4, 16, 128), BF16),
            pltpu.VMEM((32, 64, 128), BF16),
            pltpu.VMEM((1024, 128), F32),
            pltpu.VMEM((64, 16, 128), BF16),
            pltpu.VMEM((NY, NX, 2, 4, 16, 128), BF16),
            pltpu.VMEM((128, 16, 128), BF16),
            pltpu.VMEM((128, 256), BF16),
            pltpu.VMEM((64, 256), BF16),
            pltpu.VMEM((4096, 128), F32),
            pltpu.VMEM((4096, 128), F32),
            pltpu.VMEM((2048, 128), F32),
            pltpu.VMEM((2, 4, 4, 4, 16, 128), F32),
            pltpu.VMEM((16, 64, 128), F32),
            pltpu.VMEM((128, 128), F32),
            pltpu.VMEM((3, 4, 4, 16, 128), F32),
            pltpu.VMEM((3, 4, 4, 16, 128), F32),
            pltpu.VMEM((4, 4, 16, 128), F32),
            pltpu.VMEM((4, 4, 16, 128), F32),
            pltpu.VMEM((2, 4, 4, 16, 128), F32),
            pltpu.VMEM((2, 2, 2, 64, 128), F32),
            pltpu.VMEM((2, 2, 64, 128), F32),
            pltpu.VMEM((2, 64, 128), F32),
            pltpu.VMEM((2, 2, 64, 128), F32),
            dma((15,)),
            dma((CHUNKS,)),
            dma((2, 4, 2)),
            dma((2, 4, 2)),
            dma((4, 2)),
            dma((2, 4)),
            dma((2, 4)),
            dma((2, 4)),
            dma((2, 4)),
            dma((2, 4)),
            dma((2, 3)),
            dma((2, 3)),
            dma((2, 4)),
            dma((2, 4)),
        ],
        compiler_params=pltpu.CompilerParams(
            collective_id=0, has_side_effects=True, vmem_limit_bytes=VMEM_BYTES
        ),
    )(*operands)


def solution(mesh):
    placed = (
        P("row", "col", None, None, None),
        P("row", "col", None),
        P("row", "col", None),
        P("row", "col"),
        P("row", "col"),
        P(),
        P(None, ("row", "col")),
    )
    return jax.shard_map(
        on_device,
        mesh=mesh,
        in_specs=placed,
        out_specs=(P(None, ("row", "col")), P("row", "col")),
        check_vma=False,
    )
```

time: 301 us -> 45.7 us (0.15)
  waiting for transfers between devices: 194 us -> 0 us
  Pallas kernels: 0 us -> 41.3 us
  other arithmetic: 26.7 us -> 0 us
  blocking collectives: 24.2 us -> 0 us
  matrix products: 17.9 us -> 0 us
  local copies, waits for them, and re-layouts: 20.6 us -> 2.95 us
  between operations: 15.2 us -> 1.29 us
    unnamed x4 -> x0, waiting for transfers between devices: 101 us -> none
    reduce_scatter x1 -> x0, waiting for transfers between devices: 91.1 us -> none  [on_device(): lax.psum_scatter(value_acc.reshape(REWARDS, sb_row * BLK), 'col', scatter...]
    pallas_call x0 -> x1, Pallas kernels: none -> 41.3 us  [on_device(): pl.pallas_call(kernel, out_shape=(jax.ShapeDtypeStruct((16, 1024), F32),...]
    all_gather x1 -> x0, blocking collectives: 24.2 us -> none  [on_device(): reward_full = lax.all_gather(reward_table, 'row', axis=0, tiled=True)]
    dot_general x10 -> x0, matrix products: 17.9 us -> none  [the longest x5 9.6 us: visit(): jnp.einsum('kgc,grc->kgr', picked, block_set, preferred_element_type=jnp....]
    scatter-add x10 -> x0, other arithmetic: 17.1 us -> none  [the longest x5 8.55 us: visit(): grad_now = grad_now.at[:, col_set].add(product * live_mask)]
    gather x11 -> x0, local copies, waits for them, and re-layouts: 12.8 us -> none  [the longest x5 9.09 us: visit(): weights = jnp.take(weight_cells, row_set, axis=1)]
    and x11 -> x0, other arithmetic: 7.94 us -> none  [the longest x5 3.64 us: visit(): picked = jnp.take(reward_cells, col_set, axis=1)]
  transfers between devices with their start and end apart: 3 -> 0, of which waited for: 3 -> 0; matrix products, arithmetic and copies ran while one was open for 10% -> 0% of each run, Pallas kernels for 0% -> 0%
where the time goes in v2:
time: 45.7 us; the launch traced here: 45.5 us
  Pallas kernels  41.3 us (90%)
  local copies, waits for them, and re-layouts  2.95 us (6%)
  between operations  1.29 us (3%)
    pallas_call x1, Pallas kernels, on_device(): pl.pallas_call(kernel, out_shape=(jax.ShapeDtypeStruct((16, 1024), F32),...  41.3 us
    unnamed x2, local copies, waits for them, and re-layouts  2.95 us

profile of v2, /device:TPU:1, one launch (start us, length us, event | category | flops | bytes accessed | tf_op | source)
XLA Modules:
  0.0 45.5 jit_solution(18134407533978915321)
XLA Ops:
  1.3 41.3 %shard_map.86 = (f32[16,1024]{1,0:T(8,128)}, f32[2,8192]{1,0:T(2,128)}) custom-call(bf16[1,1,256,128,128]{4,3,2,1,0:T(8,128)(2,1)} %blocks.1, s32[1,1,256]{2,1,0:T(1,128)} %slot_rows.1, s32[1,1,256]{2,1,0:T(1,128)} %slot_cols.1, s32[1,1]{1,0:T(1,128)S(6)} %copy.11.counts, bf16[4,8192]{1,0:T(4,128)(2,1)} %table.1, s32[16]{0:T(128)} %reward_cols.1, ...), custom_call_target="tpu_custom_call" | custom-call | tf_op jit(solution)/shard_map/pallas_call | solution.py:339
  42.6 1.5 %copy.12 = f32[16,1024]{1,0:T(8,128)} copy(f32[16,1024]{1,0:T(8,128)} %get-tuple-element.4) | data formatting | bytes 131072
  44.0 1.5 %copy.13 = f32[2,8192]{1,0:T(2,128)} copy(f32[2,8192]{1,0:T(2,128)} %get-tuple-element.5) | data formatting | bytes 131072

commit v3 on v2

--- a/solution.py
+++ b/solution.py
@@ -14,7 +14,7 @@
 NZ = 8
 NX = 4
 NY = 4
-VMEM_BYTES = 62 << 20
+VMEM_BYTES = 48 << 20
 UNROLL = 64
 CHUNKS = 8
 
@@ -76,6 +76,11 @@
 
     def at_z(step):
         return lax.rem(z + NZ + step, NZ)
+
+    semaphore = pltpu.get_barrier_semaphore()
+    peers = [along_z(2), along_z(-2), along_z(1), along_z(-1)] + plane_peers(z, x, y, core)
+    for peer in peers:
+        pl.semaphore_signal(semaphore, inc=1, device_id=peer, device_id_type=MESH)
 
     loads = [
         pltpu.make_async_copy(table, tab, load_sem.at[0]),
@@ -99,10 +104,6 @@
     ]
     for load in loads[:1] + cot_loads + loads[1:] + block_loads:
         load.start()
-    semaphore = pltpu.get_barrier_semaphore()
-    peers = [along_z(2), along_z(-2), along_z(1), along_z(-1)] + plane_peers(z, x, y, core)
-    for peer in peers:
-        pl.semaphore_signal(semaphore, inc=1, device_id=peer, device_id_type=MESH)
     loads[0].wait()
     for j in range(64):
         tabf[pl.ds(j, 4, stride=64), :] = tab[:, j * 128 : (j + 1) * 128].astype(F32)
@@ -174,14 +175,53 @@
             if half == way:
                 reward_copy(way, 3, half, False).start()
 
+    for load in block_loads:
+        load.wait()
+
+    for way in (0, 1):
+        for half in (0, 1):
+            reward_copy(way, 0, half, True).wait_recv()
+            reward_copy(way, 2, half, True).wait_recv()
+        reward_copy(way, 3, way, True).wait_recv()
+    for k in range(16):
+        sel[k * 64 : (k + 1) * 64] = full[picks_s[k]].astype(F32)
+    for j in range(64):
+        rew[j] = sel[pl.ds(j, 16, stride=64), :].astype(BF16)
+
+    @pl.loop(0, 256, step=UNROLL)
+    def _(start):
+        for u in range(0, UNROLL, 2):
+            s = start + u
+            pair = stored[pl.ds(s, 2)].reshape(256, 128)
+            left = jnp.concatenate([rew[cols_s[0, 0, s]], rew[cols_s[0, 0, s + 1]]], axis=0)
+            out = lax.dot_general(left, pair, NT, preferred_element_type=F32)
+            at = pl.multiple_of(s * 16, 32)
+            forward[pl.ds(at, 16), :] = out[:16, :128]
+            forward[pl.ds(at + 16, 16), :] = out[16:, 128:]
+
+    for k in range(16):
+        vsum[k * 128 : (k + 1) * 128] = slot_sums(hot_rows[...], forward, k)
+    for i in range(128):
+        vtile[i >> 6, (i >> 4) & 3, (i >> 2) & 3, i & 3] = vsum[pl.ds(i, 16, stride=128), :]
+
+    value_first = []
+    for i in range(1, NX):
+        tx = lax.rem(x + i, NX)
+        ty = lax.rem(y + i, NY)
+        value_first.append(
+            remote(vtile.at[0, tx], abuf.at[i - 1], vsend.at[0, i - 1], vrecv.at[0, i - 1], device(z, tx, y, core))
+        )
+        value_first.append(
+            remote(vtile.at[1, ty], bbuf.at[i - 1], vsend.at[1, i - 1], vrecv.at[1, i - 1], device(z, x, ty, core))
+        )
+    for copy in value_first:
+        copy.start()
+
     for i in range(1, NX):
         row, column = w.at[lax.rem(y + NY - i, NY), :, 0], w.at[:, lax.rem(x + NX - i, NX), 1]
         remote(row, row, qsend.at[0, i], qrecv.at[0, i], partner).wait_recv()
         remote(column, column, qsend.at[1, i], qrecv.at[1, i], partner).wait_recv()
     wf[...] = w[...].reshape(wf.shape)
-    for load in block_loads:
-        load.wait()
-
     zero = jnp.zeros((16, 128), BF16)
 
     @pl.loop(0, 256, step=UNROLL)
@@ -229,45 +269,6 @@
             copy(way).start()
 
     for way in (0, 1):
-        for half in (0, 1):
-            reward_copy(way, 0, half, True).wait_recv()
-            reward_copy(way, 2, half, True).wait_recv()
-        reward_copy(way, 3, way, True).wait_recv()
-    for k in range(16):
-        sel[k * 64 : (k + 1) * 64] = full[picks_s[k]].astype(F32)
-    for j in range(64):
-        rew[j] = sel[pl.ds(j, 16, stride=64), :].astype(BF16)
-
-    @pl.loop(0, 256, step=UNROLL)
-    def _(start):
-        for u in range(0, UNROLL, 2):
-            s = start + u
-            pair = stored[pl.ds(s, 2)].reshape(256, 128)
-            left = jnp.concatenate([rew[cols_s[0, 0, s]], rew[cols_s[0, 0, s + 1]]], axis=0)
-            out = lax.dot_general(left, pair, NT, preferred_element_type=F32)
-            at = pl.multiple_of(s * 16, 32)
-            forward[pl.ds(at, 16), :] = out[:16, :128]
-            forward[pl.ds(at + 16, 16), :] = out[16:, 128:]
-
-    for k in range(16):
-        vsum[k * 128 : (k + 1) * 128] = slot_sums(hot_rows[...], forward, k)
-    for i in range(128):
-        vtile[i >> 6, (i >> 4) & 3, (i >> 2) & 3, i & 3] = vsum[pl.ds(i, 16, stride=128), :]
-
-    value_first = []
-    for i in range(1, NX):
-        tx = lax.rem(x + i, NX)
-        ty = lax.rem(y + i, NY)
-        value_first.append(
-            remote(vtile.at[0, tx], abuf.at[i - 1], vsend.at[0, i - 1], vrecv.at[0, i - 1], device(z, tx, y, core))
-        )
-        value_first.append(
-            remote(vtile.at[1, ty], bbuf.at[i - 1], vsend.at[1, i - 1], vrecv.at[1, i - 1], device(z, x, ty, core))
-        )
-    for copy in value_first:
-        copy.start()
-
-    for way in (0, 1):
         mid_copy(way).wait_recv()
         far_copy(way).wait_recv()
         s = sign_of(way)
@@ -336,6 +337,10 @@
 def on_device(*operands):
     vmem = pl.BlockSpec(memory_space=pltpu.VMEM)
     dma = pltpu.SemaphoreType.DMA
+    operands = [
+        operand if operand.size == 1 else pltpu.with_memory_space_constraint(operand, pltpu.HBM)
+        for operand in operands
+    ]
     return pl.pallas_call(
         kernel,
         out_shape=(jax.ShapeDtypeStruct((16, 1024), F32), jax.ShapeDtypeStruct((2, 8192), F32)),

time: 45.7 us -> 41.5 us (0.908)
  Pallas kernels: 41.3 us -> 38.9 us
  local copies, waits for them, and re-layouts: 2.95 us -> 1.26 us
    pallas_call x1, Pallas kernels: 41.3 us -> 38.9 us  [on_device(): pl.pallas_call(kernel, out_shape=(jax.ShapeDtypeStruct((16, 1024), F32),...]
    unnamed x2, local copies, waits for them, and re-layouts: 2.95 us -> 1.26 us
where the time goes in v3:
time: 41.5 us; the launch traced here: 41.4 us
  Pallas kernels  38.9 us (94%)
  between operations  1.29 us (3%)
  local copies, waits for them, and re-layouts  1.26 us (3%)
    pallas_call x1, Pallas kernels, on_device(): pl.pallas_call(kernel, out_shape=(jax.ShapeDtypeStruct((16, 1024), F32),...  38.9 us
    unnamed x2, local copies, waits for them, and re-layouts  1.26 us

profile of v3, /device:TPU:1, one launch (start us, length us, event | category | flops | bytes accessed | tf_op | source)
XLA Modules:
  0.0 41.4 jit_solution(10746578553034724557)
XLA Ops:
  1.3 38.9 %shard_map.86 = (f32[16,1024]{1,0:T(8,128)S(1)}, f32[2,8192]{1,0:T(2,128)S(1)}) custom-call(bf16[1,1,256,128,128]{4,3,2,1,0:T(8,128)(2,1)} %blocks.1, s32[1,1,256]{2,1,0:T(1,128)} %slot_rows.1, s32[1,1,256]{2,1,0:T(1,128)} %slot_cols.1, s32[1,1]{1,0:T(1,128)S(6)} %copy.11.counts, bf16[4,8192]{1,0:T(4,128)(2,1)} %table.1, s32[16]{0:T(128)} %reward_cols.1, ...), custom_call_target="tpu_custom_call" | custom-call | tf_op jit(solution)/shard_map/pallas_call | solution.py:344
  40.2 0.6 %copy.12 = f32[16,1024]{1,0:T(8,128)} copy(f32[16,1024]{1,0:T(8,128)S(1)} %get-tuple-element.4) | data formatting | bytes 131072
  40.8 0.6 %copy.13 = f32[2,8192]{1,0:T(2,128)} copy(f32[2,8192]{1,0:T(2,128)S(1)} %get-tuple-element.5) | data formatting | bytes 131072

commit v4 on v3

--- a/solution.py
+++ b/solution.py
@@ -15,7 +15,8 @@
 NX = 4
 NY = 4
 VMEM_BYTES = 48 << 20
-UNROLL = 64
+UNROLL = 128
+TURN = 32
 CHUNKS = 8
 
 
@@ -61,7 +62,7 @@
 
 def kernel(
     blocks, slot_rows, slot_cols, counts, table, reward_cols, cot, value_out, grad_out,
-    stored, rows_s, cols_s, count_s, picks_s, rows_v, cols_v,
+    stored, turned, rows_s, cols_s, count_s, picks_s, rows_v, cols_v,
     tab, tabf, own_cot, full, sel, rew, w, wf, hot_rows, hot_cols,
     adjoint, forward, vsum, vtile, grads, gsum,
     abuf, bbuf, asum, bsum, fin, near, mid, far, relay,
@@ -150,6 +151,15 @@
     hot_rows[...] = one_hot(rows_v[0], 128, live, block_row)
     hot_cols[...] = one_hot(cols_v[0], 64, live, lambda at: at)
 
+    def turn(start, stop):
+        @pl.loop(start, stop, step=TURN)
+        def _(at):
+            for u in range(TURN):
+                turned[at + u] = stored[at + u].T
+
+    for load in block_loads[: CHUNKS // 2]:
+        load.wait()
+    turn(0, 128)
     remote(own_cot.at[0], w.at[y, x, 1 - core], psend.at[0, 0], precv.at[1 - core, 0], partner).wait_recv()
     for i in range(1, NX):
         for half in range(2):
@@ -168,15 +178,15 @@
     for copy in second:
         copy.start()
 
+    for load in block_loads[CHUNKS // 2 :]:
+        load.wait()
+    turn(128, 256)
     for half in (0, 1):
         for way in (0, 1):
             reward_copy(way, 1, half, True).wait_recv()
             reward_copy(way, 2, half, False).start()
             if half == way:
                 reward_copy(way, 3, half, False).start()
-
-    for load in block_loads:
-        load.wait()
 
     for way in (0, 1):
         for half in (0, 1):
@@ -188,56 +198,51 @@
     for j in range(64):
         rew[j] = sel[pl.ds(j, 16, stride=64), :].astype(BF16)
 
+    zero = jnp.zeros((16, 128), BF16)
+
+    def spread(a, b):
+        return jnp.concatenate(
+            [jnp.concatenate([a, zero], axis=1), jnp.concatenate([zero, b], axis=1)], axis=0
+        )
+
     @pl.loop(0, 256, step=UNROLL)
     def _(start):
         for u in range(0, UNROLL, 2):
             s = start + u
-            pair = stored[pl.ds(s, 2)].reshape(256, 128)
-            left = jnp.concatenate([rew[cols_s[0, 0, s]], rew[cols_s[0, 0, s + 1]]], axis=0)
-            out = lax.dot_general(left, pair, NT, preferred_element_type=F32)
-            at = pl.multiple_of(s * 16, 32)
-            forward[pl.ds(at, 16), :] = out[:16, :128]
-            forward[pl.ds(at + 16, 16), :] = out[16:, 128:]
-
-    for k in range(16):
-        vsum[k * 128 : (k + 1) * 128] = slot_sums(hot_rows[...], forward, k)
-    for i in range(128):
-        vtile[i >> 6, (i >> 4) & 3, (i >> 2) & 3, i & 3] = vsum[pl.ds(i, 16, stride=128), :]
-
-    value_first = []
-    for i in range(1, NX):
-        tx = lax.rem(x + i, NX)
-        ty = lax.rem(y + i, NY)
-        value_first.append(
-            remote(vtile.at[0, tx], abuf.at[i - 1], vsend.at[0, i - 1], vrecv.at[0, i - 1], device(z, tx, y, core))
-        )
-        value_first.append(
-            remote(vtile.at[1, ty], bbuf.at[i - 1], vsend.at[1, i - 1], vrecv.at[1, i - 1], device(z, x, ty, core))
-        )
-    for copy in value_first:
-        copy.start()
+            left = spread(rew[cols_s[0, 0, s]], rew[cols_s[0, 0, s + 1]])
+            pair = turned[pl.ds(s, 2)].reshape(256, 128)
+            forward[pl.ds(pl.multiple_of(s * 16, 32), 32), :] = jnp.dot(left, pair, preferred_element_type=F32)
+
+    value_first = ([], [])
+    for part in (0, 1):
+        for k in range(part * 8, part * 8 + 8):
+            vsum[k * 128 : (k + 1) * 128] = slot_sums(hot_rows[...], forward, k)
+        for i in range(128):
+            vtile[part, i >> 6, (i >> 4) & 3, (i >> 2) & 3, i & 3] = vsum[pl.ds(part * 1024 + i, 8, stride=128), :]
+        for i in range(1, NX):
+            tx = lax.rem(x + i, NX)
+            ty = lax.rem(y + i, NY)
+            for half, src, dst, peer in (
+                (0, vtile.at[part, 0, tx], abuf, device(z, tx, y, core)),
+                (1, vtile.at[part, 1, ty], bbuf, device(z, x, ty, core)),
+            ):
+                at = (part, half, i - 1)
+                value_first[part].append(remote(src, dst.at[part, i - 1], vsend.at[at], vrecv.at[at], peer))
+        for copy in value_first[part]:
+            copy.start()
 
     for i in range(1, NX):
         row, column = w.at[lax.rem(y + NY - i, NY), :, 0], w.at[:, lax.rem(x + NX - i, NX), 1]
         remote(row, row, qsend.at[0, i], qrecv.at[0, i], partner).wait_recv()
         remote(column, column, qsend.at[1, i], qrecv.at[1, i], partner).wait_recv()
     wf[...] = w[...].reshape(wf.shape)
-    zero = jnp.zeros((16, 128), BF16)
-
     @pl.loop(0, 256, step=UNROLL)
     def _(start):
         for u in range(0, UNROLL, 2):
             s = start + u
+            left = spread(wf[lax.div(rows_s[0, 0, s], 2)], wf[lax.div(rows_s[0, 0, s + 1], 2)])
             pair = stored[pl.ds(s, 2)].reshape(256, 128)
-            w0 = wf[lax.div(rows_s[0, 0, s], 2)]
-            w1 = wf[lax.div(rows_s[0, 0, s + 1], 2)]
-            left = jnp.concatenate(
-                [jnp.concatenate([w0, zero], axis=1), jnp.concatenate([zero, w1], axis=1)], axis=0
-            )
             adjoint[pl.ds(pl.multiple_of(s * 16, 32), 32), :] = jnp.dot(left, pair, preferred_element_type=F32)
-
-    for k in range(16):
-        grads[k] = slot_sums(hot_cols[...], adjoint, k)
 
     def sign_of(way):
         return 1 if way == 0 else -1
@@ -264,9 +269,54 @@
         s = sign_of(way)
         return remote(relay.at[way], near.at[1, way], zsend.at[way, 3], zrecv.at[way, 3], along_z(2 * s))
 
-    for copy in (far_copy, mid_copy, near_copy):
-        for way in (0, 1):
+    for step, ready in (
+        (3, [(mid_copy, 0)]), (-3, [(mid_copy, 1)]), (4, [(far_copy, 0), (far_copy, 1)]),
+        (1, [(near_copy, 0)]), (-1, [(near_copy, 1)]), (2, []), (-2, []), (0, []),
+    ):
+        for r in (0, 1):
+            k = at_z(step) * 2 + r
+            grads[k] = slot_sums(hot_cols[...], adjoint, k)
+        for copy, way in ready:
             copy(way).start()
+
+    value_second = []
+    last = []
+    for part in (0, 1):
+        for copy in value_first[part]:
+            copy.wait_recv()
+        asum[part] = vtile[part, 0, x] + abuf[part, 0] + abuf[part, 1] + abuf[part, 2]
+        bsum[part] = vtile[part, 1, y] + bbuf[part, 0] + bbuf[part, 1] + bbuf[part, 2]
+        second_copies = []
+        for i in range(1, NX):
+            ty = lax.rem(y + i, NY)
+            tx = lax.rem(x + i, NX)
+            for half, src, peer in ((0, asum.at[part, ty], device(z, x, ty, 0)), (1, bsum.at[part, tx], device(z, tx, y, 1))):
+                second_copies.append(
+                    remote(src, fin.at[part, core, i], fsend.at[part, half, i], frecv.at[part, core, i], peer)
+                )
+        for copy in second_copies:
+            copy.start()
+        value_second += second_copies
+
+        @pl.when(core == 0)
+        def _():
+            remote(
+                bsum.at[part, x], fin.at[part, core, 0], fsend.at[part, 0, 0], frecv.at[part, core, 0], partner
+            ).start()
+            fin[part, core, 0] = asum[part, y]
+
+        @pl.when(core == 1)
+        def _():
+            remote(
+                asum.at[part, y], fin.at[part, core, 0], fsend.at[part, 0, 0], frecv.at[part, core, 0], partner
+            ).start()
+            fin[part, core, 0] = bsum[part, x]
+
+        last.append(
+            remote(
+                asum.at[part, 0], fin.at[part, 1 - core, 0], fsend.at[part, 0, 0], frecv.at[part, 1 - core, 0], partner
+            )
+        )
 
     for way in (0, 1):
         mid_copy(way).wait_recv()
@@ -276,33 +326,18 @@
         relay[way, way] = relay[way, way] + far[way]
         relay_copy(way).start()
 
-    for copy in value_first:
-        copy.wait_recv()
-    asum[...] = vtile[0, x] + abuf[0] + abuf[1] + abuf[2]
-    bsum[...] = vtile[1, y] + bbuf[0] + bbuf[1] + bbuf[2]
-
-    value_second = []
-    for i in range(1, NX):
-        ty = lax.rem(y + i, NY)
-        tx = lax.rem(x + i, NX)
-        value_second.append(
-            remote(asum.at[ty], fin.at[core, i], fsend.at[0, i], frecv.at[core, i], device(z, x, ty, 0))
-        )
-        value_second.append(
-            remote(bsum.at[tx], fin.at[core, i], fsend.at[1, i], frecv.at[core, i], device(z, tx, y, 1))
-        )
-    for copy in value_second:
-        copy.start()
-
-    @pl.when(core == 0)
-    def _():
-        remote(bsum.at[x], fin.at[core, 0], fsend.at[0, 0], frecv.at[core, 0], partner).start()
-        fin[core, 0] = asum[y]
-
-    @pl.when(core == 1)
-    def _():
-        remote(asum.at[y], fin.at[core, 0], fsend.at[0, 0], frecv.at[core, 0], partner).start()
-        fin[core, 0] = bsum[x]
+    for part in (0, 1):
+        last[part].wait_recv()
+        for c in range(2):
+            for i in range(1, NX):
+                remote(
+                    asum.at[part, 0], fin.at[part, c, i], fsend.at[part, 0, i], frecv.at[part, c, i], partner
+                ).wait_recv()
+        for t in range(8):
+            p, h = t % 2, t // 2
+            value_out[part * 8 : part * 8 + 8, t * 128 : (t + 1) * 128] = (
+                fin[part, p, 0, h] + fin[part, p, 1, h] + fin[part, p, 2, h] + fin[part, p, 3, h]
+            )
 
     for way in (0, 1):
         near_copy(way).wait_recv()
@@ -313,15 +348,6 @@
         )
     for j in range(64):
         grad_out[:, j * 128 : (j + 1) * 128] = gsum[pl.ds(j, 2, stride=64), :]
-
-    last = remote(asum.at[0], fin.at[1 - core, 0], fsend.at[0, 0], frecv.at[1 - core, 0], partner)
-    last.wait_recv()
-    for c in range(2):
-        for i in range(1, NX):
-            remote(asum.at[0], fin.at[c, i], fsend.at[0, i], frecv.at[c, i], partner).wait_recv()
-    for t in range(8):
-        p, h = t % 2, t // 2
-        value_out[:, t * 128 : (t + 1) * 128] = fin[p, 0, h] + fin[p, 1, h] + fin[p, 2, h] + fin[p, 3, h]
 
     for way in (0, 1):
         for half in (0, 1):
@@ -330,8 +356,32 @@
         reward_copy(way, 3, way, False).wait_send()
         for copy in (far_copy, mid_copy, near_copy, relay_copy):
             copy(way).wait_send()
-    for copy in first + second + value_first + value_second + [last]:
+    for copy in first + second + value_first[0] + value_first[1] + value_second + last:
         copy.wait_send()
+
+
+def hand_on_kernel(value, grad, value_out, grad_out, sem):
+    copies = [
+        pltpu.make_async_copy(value, value_out, sem.at[0]),
+        pltpu.make_async_copy(grad, grad_out, sem.at[1]),
+    ]
+    for copy in copies:
+        copy.start()
+    for copy in copies:
+        copy.wait()
+
+
+def hand_on(value, grad):
+    vmem = pl.BlockSpec(memory_space=pltpu.VMEM)
+    anywhere = pl.BlockSpec(memory_space=pl.ANY)
+    return pl.pallas_call(
+        hand_on_kernel,
+        out_shape=(jax.ShapeDtypeStruct((16, 1024), F32), jax.ShapeDtypeStruct((2, 8192), F32)),
+        in_specs=[vmem, vmem],
+        out_specs=(anywhere, anywhere),
+        scratch_shapes=[pltpu.SemaphoreType.DMA((2,))],
+        compiler_params=pltpu.CompilerParams(vmem_limit_bytes=VMEM_BYTES),
+    )(value, grad)
 
 
 def on_device(*operands):
@@ -341,12 +391,13 @@
         operand if operand.size == 1 else pltpu.with_memory_space_constraint(operand, pltpu.HBM)
         for operand in operands
     ]
-    return pl.pallas_call(
+    value, grad = pl.pallas_call(
         kernel,
         out_shape=(jax.ShapeDtypeStruct((16, 1024), F32), jax.ShapeDtypeStruct((2, 8192), F32)),
         in_specs=[pl.BlockSpec(memory_space=pltpu.HBM)] * 7,
         out_specs=(vmem, vmem),
         scratch_shapes=[
+            pltpu.VMEM((256, 128, 128), BF16),
             pltpu.VMEM((256, 128, 128), BF16),
             pltpu.SMEM((1, 1, 256), jnp.int32),
             pltpu.SMEM((1, 1, 256), jnp.int32),
@@ -367,14 +418,14 @@
             pltpu.VMEM((4096, 128), F32),
             pltpu.VMEM((4096, 128), F32),
             pltpu.VMEM((2048, 128), F32),
-            pltpu.VMEM((2, 4, 4, 4, 16, 128), F32),
+            pltpu.VMEM((2, 2, 4, 4, 4, 8, 128), F32),
             pltpu.VMEM((16, 64, 128), F32),
             pltpu.VMEM((128, 128), F32),
-            pltpu.VMEM((3, 4, 4, 16, 128), F32),
-            pltpu.VMEM((3, 4, 4, 16, 128), F32),
-            pltpu.VMEM((4, 4, 16, 128), F32),
-            pltpu.VMEM((4, 4, 16, 128), F32),
-            pltpu.VMEM((2, 4, 4, 16, 128), F32),
+            pltpu.VMEM((2, 3, 4, 4, 8, 128), F32),
+            pltpu.VMEM((2, 3, 4, 4, 8, 128), F32),
+            pltpu.VMEM((2, 4, 4, 8, 128), F32),
+            pltpu.VMEM((2, 4, 4, 8, 128), F32),
+            pltpu.VMEM((2, 2, 4, 4, 8, 128), F32),
             pltpu.VMEM((2, 2, 2, 64, 128), F32),
             pltpu.VMEM((2, 2, 64, 128), F32),
             pltpu.VMEM((2, 64, 128), F32),
@@ -389,15 +440,16 @@
             dma((2, 4)),
             dma((2, 4)),
             dma((2, 4)),
-            dma((2, 3)),
-            dma((2, 3)),
-            dma((2, 4)),
-            dma((2, 4)),
+            dma((2, 2, 3)),
+            dma((2, 2, 3)),
+            dma((2, 2, 4)),
+            dma((2, 2, 4)),
         ],
         compiler_params=pltpu.CompilerParams(
             collective_id=0, has_side_effects=True, vmem_limit_bytes=VMEM_BYTES
         ),
     )(*operands)
+    return hand_on(value, grad)
 
 
 def solution(mesh):

time: 41.5 us -> 38.7 us (0.933)
  Pallas kernels: 38.9 us -> 37.3 us
  local copies, waits for them, and re-layouts: 1.26 us -> 0 us
    pallas_call x1, Pallas kernels: 38.9 us -> 36.7 us  [on_device(): pl.pallas_call(kernel, out_shape=(jax.ShapeDtypeStruct((16, 1024), F32),...]
    unnamed x2 -> x0, local copies, waits for them, and re-layouts: 1.26 us -> none
    pallas_call x0 -> x1, Pallas kernels: none -> 0.67 us  [hand_on(): pl.pallas_call(hand_on_kernel, out_shape=(jax.ShapeDtypeStruct((16, 1024)...]
where the time goes in v4:
time: 38.7 us; the launch traced here: 38.6 us
  Pallas kernels  37.3 us (96%)
  between operations  1.28 us (3%)
    pallas_call x1, Pallas kernels, on_device(): pl.pallas_call(kernel, out_shape=(jax.ShapeDtypeStruct((16, 1024), F32),...  36.7 us

profile of v4, /device:TPU:1, one launch (start us, length us, event | category | flops | bytes accessed | tf_op | source)
XLA Modules:
  0.0 38.6 jit_solution(13503691562310980123)
XLA Ops:
  1.3 36.7 %shard_map.86 = (f32[16,1024]{1,0:T(8,128)S(1)}, f32[2,8192]{1,0:T(2,128)S(1)}) custom-call(bf16[1,1,256,128,128]{4,3,2,1,0:T(8,128)(2,1)} %blocks.1, s32[1,1,256]{2,1,0:T(1,128)} %slot_rows.1, s32[1,1,256]{2,1,0:T(1,128)} %slot_cols.1, s32[1,1]{1,0:T(1,128)S(6)} %copy.9.counts, bf16[4,8192]{1,0:T(4,128)(2,1)} %table.1, s32[16]{0:T(128)} %reward_cols.1, ...), custom_call_target="tpu_custom_call" | custom-call | tf_op jit(solution)/shard_map/pallas_call | solution.py:394
  38.0 0.7 %shard_map.87 = (f32[16,1024]{1,0:T(8,128)}, f32[2,8192]{1,0:T(2,128)}) custom-call(f32[16,1024]{1,0:T(8,128)S(1)} %get-tuple-element.4.value, f32[2,8192]{1,0:T(2,128)S(1)} %get-tuple-element.5.grad), custom_call_target="tpu_custom_call" | custom-call | tf_op jit(solution)/shard_map/pallas_call | solution.py:377

commit v5 on v4

--- a/solution.py
+++ b/solution.py
@@ -157,9 +157,6 @@
             for u in range(TURN):
                 turned[at + u] = stored[at + u].T
 
-    for load in block_loads[: CHUNKS // 2]:
-        load.wait()
-    turn(0, 128)
     remote(own_cot.at[0], w.at[y, x, 1 - core], psend.at[0, 0], precv.at[1 - core, 0], partner).wait_recv()
     for i in range(1, NX):
         for half in range(2):
@@ -178,15 +175,16 @@
     for copy in second:
         copy.start()
 
-    for load in block_loads[CHUNKS // 2 :]:
-        load.wait()
-    turn(128, 256)
     for half in (0, 1):
         for way in (0, 1):
             reward_copy(way, 1, half, True).wait_recv()
             reward_copy(way, 2, half, False).start()
             if half == way:
                 reward_copy(way, 3, half, False).start()
+
+    for load in block_loads:
+        load.wait()
+    turn(0, 256)
 
     for way in (0, 1):
         for half in (0, 1):

time: 38.7 us -> 36.9 us (0.953)
  Pallas kernels: 37.3 us -> 35.5 us
    pallas_call x1, Pallas kernels: 36.7 us -> 34.8 us  [on_device(): pl.pallas_call(kernel, out_shape=(jax.ShapeDtypeStruct((16, 1024), F32),...]
where the time goes in v5:
time: 36.9 us; the launch traced here: 36.8 us
  Pallas kernels  35.5 us (96%)
  between operations  1.28 us (3%)
    pallas_call x1, Pallas kernels, on_device(): pl.pallas_call(kernel, out_shape=(jax.ShapeDtypeStruct((16, 1024), F32),...  34.8 us

profile of v5, /device:TPU:1, one launch (start us, length us, event | category | flops | bytes accessed | tf_op | source)
XLA Modules:
  0.0 36.8 jit_solution(13537570098866515946)
XLA Ops:
  1.3 34.8 %shard_map.86 = (f32[16,1024]{1,0:T(8,128)S(1)}, f32[2,8192]{1,0:T(2,128)S(1)}) custom-call(bf16[1,1,256,128,128]{4,3,2,1,0:T(8,128)(2,1)} %blocks.1, s32[1,1,256]{2,1,0:T(1,128)} %slot_rows.1, s32[1,1,256]{2,1,0:T(1,128)} %slot_cols.1, s32[1,1]{1,0:T(1,128)S(6)} %copy.9.counts, bf16[4,8192]{1,0:T(4,128)(2,1)} %table.1, s32[16]{0:T(128)} %reward_cols.1, ...), custom_call_target="tpu_custom_call" | custom-call | tf_op jit(solution)/shard_map/pallas_call | solution.py:392
  36.1 0.7 %shard_map.87 = (f32[16,1024]{1,0:T(8,128)}, f32[2,8192]{1,0:T(2,128)}) custom-call(f32[16,1024]{1,0:T(8,128)S(1)} %get-tuple-element.4.value, f32[2,8192]{1,0:T(2,128)S(1)} %get-tuple-element.5.grad), custom_call_target="tpu_custom_call" | custom-call | tf_op jit(solution)/shard_map/pallas_call | solution.py:375

commit v6 on v5

--- a/solution.py
+++ b/solution.py
@@ -139,41 +139,11 @@
         copy.start()
     w[y, x, core] = own_cot[core]
 
-    for load in loads[1:]:
-        load.wait()
-    live = count_s[0, 0]
-
-    def block_row(at):
-        half, a, b, t = at >> 6, (at >> 4) & 3, (at >> 2) & 3, at & 3
-        tx, ty = jnp.where(half == 0, a, b), jnp.where(half == 0, b, a)
-        return ((ty * NX + tx) * 2 + half) * 8 + t * 2 + core
-
-    hot_rows[...] = one_hot(rows_v[0], 128, live, block_row)
-    hot_cols[...] = one_hot(cols_v[0], 64, live, lambda at: at)
-
     def turn(start, stop):
         @pl.loop(start, stop, step=TURN)
         def _(at):
             for u in range(TURN):
                 turned[at + u] = stored[at + u].T
-
-    remote(own_cot.at[0], w.at[y, x, 1 - core], psend.at[0, 0], precv.at[1 - core, 0], partner).wait_recv()
-    for i in range(1, NX):
-        for half in range(2):
-            piece = w.at[lax.rem(y + NY - i * half, NY), lax.rem(x + NX - i * (1 - half), NX), half]
-            remote(own_cot.at[0], piece, psend.at[0, 0], precv.at[half, i], partner).wait_recv()
-
-    second = []
-    for i in range(1, NX):
-        row, column = w.at[y, :, 0], w.at[:, x, 1]
-        second.append(
-            remote(row, row, qsend.at[0, i], qrecv.at[0, i], device(z, x, lax.rem(y + i, NY), core))
-        )
-        second.append(
-            remote(column, column, qsend.at[1, i], qrecv.at[1, i], device(z, lax.rem(x + i, NX), y, core))
-        )
-    for copy in second:
-        copy.start()
 
     for half in (0, 1):
         for way in (0, 1):
@@ -182,9 +152,39 @@
             if half == way:
                 reward_copy(way, 3, half, False).start()
 
+    remote(own_cot.at[0], w.at[y, x, 1 - core], psend.at[0, 0], precv.at[1 - core, 0], partner).wait_recv()
+    for i in range(1, NX):
+        for half in range(2):
+            piece = w.at[lax.rem(y + NY - i * half, NY), lax.rem(x + NX - i * (1 - half), NX), half]
+            remote(own_cot.at[0], piece, psend.at[0, 0], precv.at[half, i], partner).wait_recv()
+
+    second = []
+    for i in range(1, NX):
+        row, column = w.at[y, :, 0], w.at[:, x, 1]
+        second.append(
+            remote(row, row, qsend.at[0, i], qrecv.at[0, i], device(z, x, lax.rem(y + i, NY), core))
+        )
+        second.append(
+            remote(column, column, qsend.at[1, i], qrecv.at[1, i], device(z, lax.rem(x + i, NX), y, core))
+        )
+    for copy in second:
+        copy.start()
+
     for load in block_loads:
         load.wait()
     turn(0, 256)
+
+    for load in loads[1:]:
+        load.wait()
+    live = count_s[0, 0]
+
+    def block_row(at):
+        half, a, b, t = at >> 6, (at >> 4) & 3, (at >> 2) & 3, at & 3
+        tx, ty = jnp.where(half == 0, a, b), jnp.where(half == 0, b, a)
+        return ((ty * NX + tx) * 2 + half) * 8 + t * 2 + core
+
+    hot_rows[...] = one_hot(rows_v[0], 128, live, block_row)
+    hot_cols[...] = one_hot(cols_v[0], 64, live, lambda at: at)
 
     for way in (0, 1):
         for half in (0, 1):
@@ -217,7 +217,7 @@
             vsum[k * 128 : (k + 1) * 128] = slot_sums(hot_rows[...], forward, k)
         for i in range(128):
             vtile[part, i >> 6, (i >> 4) & 3, (i >> 2) & 3, i & 3] = vsum[pl.ds(part * 1024 + i, 8, stride=128), :]
-        for i in range(1, NX):
+        for i in (2, 1, 3):
             tx = lax.rem(x + i, NX)
             ty = lax.rem(y + i, NY)
             for half, src, dst, peer in (

time: 36.9 us -> 36.2 us (0.981)
  Pallas kernels: 35.5 us -> 34.9 us
    pallas_call x1, Pallas kernels: 34.8 us -> 34.2 us  [on_device(): pl.pallas_call(kernel, out_shape=(jax.ShapeDtypeStruct((16, 1024), F32),...]
where the time goes in v6:
time: 36.2 us
  Pallas kernels  34.9 us (96%)
  between operations  1.28 us (4%)
    pallas_call x1, Pallas kernels, on_device(): pl.pallas_call(kernel, out_shape=(jax.ShapeDtypeStruct((16, 1024), F32),...  34.2 us

profile of v6, /device:TPU:1, one launch (start us, length us, event | category | flops | bytes accessed | tf_op | source)
XLA Modules:
  0.0 36.2 jit_solution(640307271492708265)
XLA Ops:
  1.3 34.2 %shard_map.86 = (f32[16,1024]{1,0:T(8,128)S(1)}, f32[2,8192]{1,0:T(2,128)S(1)}) custom-call(bf16[1,1,256,128,128]{4,3,2,1,0:T(8,128)(2,1)} %blocks.1, s32[1,1,256]{2,1,0:T(1,128)} %slot_rows.1, s32[1,1,256]{2,1,0:T(1,128)} %slot_cols.1, s32[1,1]{1,0:T(1,128)S(6)} %copy.9.counts, bf16[4,8192]{1,0:T(4,128)(2,1)} %table.1, s32[16]{0:T(128)} %reward_cols.1, ...), custom_call_target="tpu_custom_call" | custom-call | tf_op jit(solution)/shard_map/pallas_call | solution.py:392
  35.5 0.7 %shard_map.87 = (f32[16,1024]{1,0:T(8,128)}, f32[2,8192]{1,0:T(2,128)}) custom-call(f32[16,1024]{1,0:T(8,128)S(1)} %get-tuple-element.4.value, f32[2,8192]{1,0:T(2,128)S(1)} %get-tuple-element.5.grad), custom_call_target="tpu_custom_call" | custom-call | tf_op jit(solution)/shard_map/pallas_call | solution.py:375
